TPU v7x, 512 devices: a whole 4x8x8 slice. The times are simulated.
512 devices in a mesh: section: 16 (over x_hi, y), fsdp: 32 (over x_lo, z, core).
Axes of the slice: x: 4 (x_hi: 2, x_lo: 2; x = x_hi * 2 + x_lo), y: 8, z: 8, core: 2. Of those that a mesh axis runs over, the one named last changes fastest.
Arguments:
- inputs: bfloat16 [16, 8, 1024, 4096], P('section', None, 'fsdp'), may hold values from -6 to 6
- upstream: bfloat16 [8, 1024, 4096], P(None, 'fsdp'), may hold values from -6 to 6
- weights: bfloat16 [16, 4096, 512], P('section', 'fsdp')
- gain: bfloat16 [16, 4096], P('section', 'fsdp'), may hold values from 0.5 to 1.5
Outputs:
- weight_grad: float32 [16, 4096, 512], P('section', 'fsdp')
- gain_grad: float32 [16, 4096], P('section')
All inputs are finite; a program needn't handle non-finite values.
Results may differ from a plain program's by a relative error of at most 0.035.
Values may be sent and summed in bfloat16 or wider, within the bound.
No kernel may reach another device: no remote copies, remote signals or barrier semaphores. Data moves between devices by JAX's collectives and lax.ppermute only.
A program may use at most 128 MiB of HBM per device.

v0:
```python
import jax
import jax.numpy as jnp
from jax import lax
from jax.sharding import PartitionSpec as P


def passed_along(value, axis, steps):
    count = lax.axis_size(axis)
    leading, last = (max(0, -steps), min(count, count - steps))
    return lax.ppermute(value, axis, [(source, source + steps) for source in range(leading, last)])


def rope_tables(length, head):
    half_head = head // 2
    position = lax.iota(jnp.float32, length)
    freq = jnp.power(500000.0, -2.0 * lax.iota(jnp.float32, half_head) / head)
    angle = position[:, None] * freq[None, :]
    return (jnp.cos(angle), jnp.sin(angle))


def rotate(value_rows, cosine, sine_table):
    half_head = value_rows.shape[-1] // 2
    first = value_rows[..., :half_head]
    second = value_rows[..., half_head:]
    return jnp.concatenate(
        [first * cosine - second * sine_table, second * cosine + first * sine_table], axis=-1
    )


def unrotate(value_rows, cosine, sine_table):
    half_head = value_rows.shape[-1] // 2
    first = value_rows[..., :half_head]
    second = value_rows[..., half_head:]
    return jnp.concatenate(
        [first * cosine + second * sine_table, second * cosine - first * sine_table], axis=-1
    )


def contract_rows(left, right):
    return lax.dot_general(
        left, right, (((0,), (0,)), ((), ())), preferred_element_type=jnp.float32
    )


def contract_cols(left, right):
    return lax.dot_general(
        left, right, (((1,), (1,)), ((), ())), preferred_element_type=jnp.float32
    )


def on_device(inputs, upstream, weights, gain):
    sections = lax.axis_size("section")
    here = lax.axis_index("section")
    micro_count = inputs.shape[1]
    length = inputs.shape[2]
    width = inputs.shape[3]
    head = weights.shape[2] // 4
    rows_here = weights.shape[1]
    groups = lax.axis_size("fsdp")
    gain_rows = jnp.zeros((16, weights.shape[2]), jnp.bfloat16)
    gain_rows = lax.dynamic_update_slice(gain_rows, gain[0][None, :], (0, 0))
    packed = jnp.concatenate([weights[0], gain_rows], axis=0)
    gathered = lax.all_gather(packed, "fsdp", axis=0, tiled=True).reshape(
        groups, rows_here + 16, weights.shape[2]
    )
    w_full = gathered[:, :rows_here, :].reshape(groups * rows_here, weights.shape[2])
    gain_full = gathered[:, rows_here, :rows_here].reshape(groups * rows_here)
    wide_gain = gain_full.astype(jnp.float32)
    w_proj = w_full[:, : 3 * head]
    w_back = w_full[:, 3 * head :]
    xfloat = inputs[0].astype(jnp.float32)
    inv_rms = lax.rsqrt(jnp.mean(xfloat * xfloat, axis=-1, keepdims=True) + 1e-05)
    normed = xfloat * inv_rms
    hidden = (normed * wide_gain).astype(jnp.bfloat16)
    proj = jnp.dot(
        hidden.reshape(micro_count * length, width), w_proj, preferred_element_type=jnp.float32
    ).reshape(micro_count, length, 3 * head)
    cosine, sine_table = rope_tables(length, head)
    query_rows = rotate(proj[..., :head], cosine, sine_table).astype(jnp.bfloat16)
    key_rows = rotate(proj[..., head : 2 * head], cosine, sine_table).astype(jnp.bfloat16)
    value_rows = proj[..., 2 * head :].astype(jnp.bfloat16)
    score_scale = head ** (-0.5)
    causal = lax.broadcasted_iota(jnp.int32, (length, length), 0) >= lax.broadcasted_iota(
        jnp.int32, (length, length), 1
    )
    scores = (
        jnp.einsum("mqh,mkh->mqk", query_rows, key_rows, preferred_element_type=jnp.float32)
        * score_scale
    )
    probs = jax.nn.softmax(jnp.where(causal[None], scores, -1e30), axis=-1)
    probs_b = probs.astype(jnp.bfloat16)
    attended = jnp.einsum(
        "mqk,mkh->mqh", probs_b, value_rows, preferred_element_type=jnp.float32
    ).astype(jnp.bfloat16)

    def tick(tick_no, received, state):
        grad_store, proj_store, gain_acc = state
        micro = tick_no - (sections - 1 - here)
        active = jnp.logical_and(micro >= 0, micro < micro_count)
        clipped = jnp.clip(micro, 0, micro_count - 1)
        slot = jnp.clip(micro, -1, micro_count) + 1
        top_grad = lax.dynamic_index_in_dim(upstream, clipped, 0, keepdims=False)
        grad_in = jnp.where(here == sections - 1, top_grad, received)
        query_m = lax.dynamic_index_in_dim(query_rows, clipped, 0, keepdims=False)
        keys_m = lax.dynamic_index_in_dim(key_rows, clipped, 0, keepdims=False)
        values_m = lax.dynamic_index_in_dim(value_rows, clipped, 0, keepdims=False)
        probs_m = lax.dynamic_index_in_dim(probs, clipped, 0, keepdims=False)
        probs_bm = lax.dynamic_index_in_dim(probs_b, clipped, 0, keepdims=False)
        normed_m = lax.dynamic_index_in_dim(normed, clipped, 0, keepdims=False)
        inv_m = lax.dynamic_index_in_dim(inv_rms, clipped, 0, keepdims=False)
        attention_gradient = jnp.dot(grad_in, w_back, preferred_element_type=jnp.float32).astype(
            jnp.bfloat16
        )
        probability_gradient = contract_cols(attention_gradient, values_m)
        score_gradient = (
            probs_m
            * (
                probability_gradient
                - jnp.sum(probability_gradient * probs_m, axis=-1, keepdims=True)
            )
            * score_scale
        ).astype(jnp.bfloat16)
        query_gradient = jnp.dot(score_gradient, keys_m, preferred_element_type=jnp.float32)
        key_gradient = contract_rows(score_gradient, query_m)
        value_gradient = contract_rows(probs_bm, attention_gradient)
        grad_proj = jnp.concatenate(
            [
                unrotate(query_gradient, cosine, sine_table),
                unrotate(key_gradient, cosine, sine_table),
                value_gradient,
            ],
            axis=-1,
        ).astype(jnp.bfloat16)
        grad_hidden = contract_cols(grad_proj, w_proj)
        gain_term = jnp.sum(grad_hidden * normed_m, axis=0)
        grad_normed = grad_hidden * wide_gain
        grad_x = inv_m * (
            grad_normed - normed_m * jnp.mean(grad_normed * normed_m, axis=-1, keepdims=True)
        )
        grad_out = (grad_in.astype(jnp.float32) + grad_x).astype(jnp.bfloat16)
        grad_store = lax.dynamic_update_index_in_dim(grad_store, grad_in, slot, 0)
        proj_store = lax.dynamic_update_index_in_dim(proj_store, grad_proj, slot, 0)
        gain_acc = gain_acc + jnp.where(active, gain_term, 0.0)
        return (grad_out, (grad_store, proj_store, gain_acc))

    def step_loop(tick_no, carry):
        received, state = carry
        sent, state = tick(tick_no, received, state)
        received = passed_along(sent, "section", -1)
        return (received, state)

    state_start = (
        jnp.zeros((micro_count + 2, length, width), jnp.bfloat16),
        jnp.zeros((micro_count + 2, length, 3 * head), jnp.bfloat16),
        jnp.zeros((width,), jnp.float32),
    )
    total_ticks = sections + micro_count - 1
    received, state = lax.fori_loop(
        0, total_ticks - 1, step_loop, (jnp.zeros((length, width), jnp.bfloat16), state_start)
    )
    leftover, state = tick(total_ticks - 1, received, state)
    grad_store, proj_store, gain_acc = state
    tokens_all = micro_count * length
    grad_flat = grad_store[1 : micro_count + 1].reshape(tokens_all, width)
    proj_flat = proj_store[1 : micro_count + 1].reshape(tokens_all, 3 * head)
    att_flat = attended.reshape(tokens_all, head)
    shard = lax.psum_scatter(
        jnp.concatenate(
            [
                contract_rows(hidden.reshape(tokens_all, width), proj_flat),
                contract_rows(grad_flat, att_flat),
            ],
            axis=1,
        ).astype(jnp.bfloat16),
        "fsdp",
        scatter_dimension=0,
        tiled=True,
    ).astype(jnp.float32)
    gain_sum = jnp.sum(lax.all_gather(gain_acc, "fsdp", axis=0), axis=0)
    return (shard[None], gain_sum[None])


def solution(mesh):
    return jax.shard_map(
        on_device,
        mesh=mesh,
        in_specs=(
            P("section", None, "fsdp", None),
            P(None, "fsdp", None),
            P("section", "fsdp", None),
            P("section", "fsdp"),
        ),
        out_specs=(P("section", "fsdp", None), P("section", None)),
        check_vma=False,
    )
```

profile of v0, /device:TPU:4, one launch (start us, length us, event | category | flops | bytes accessed | tf_op | source)
XLA Modules:
  0.0 805.6 jit_solution(6295574927163842685)
XLA Ops:
  13.8 72.0 %all-gather.3.cloned.1.call-done = bf16[4608,512]{1,0:T(8,128)(2,1)} async-done(((bf16[144,512]{1,0:T(8,128)(2,1)}), bf16[4608,512]{1,0:T(8,128)(2,1)}) %all-gather.3.cloned.1.call-update) | async-done | bytes 4718608 | tf_op jit(solution)/shard_map/all_gather | solution.py:63
  101.4 545.1 %while.25 = (s32[]{:T(128)}, bf16[32,4096]{1,0:T(8,128)(2,1)}, bf16[10,32,4096]{2,1,0:T(8,128)(2,1)}, bf16[10,32,384]{2,1,0:T(8,128)(2,1)}, f32[4096]{0:T(1024)S...) while((s32[]{:T(128)}, bf16[32,4096]{1,0:T(8,128)(2,1)}, ...), condition=%wide.region_7.8_spmd.clone.clone.clone.clone, body=%wide.region_3.7_spmd.clone.clone.clone.clone.sunk | while | flops 137027552 | bytes 10679635 | solution.py:158
  113.3 5.0 collective-permute-start
  119.0 5.5 collective-permute-done
  137.0 7.9 collective-permute-start
  145.6 4.7 collective-permute-done
  162.9 7.9 collective-permute-start
  171.5 3.8 collective-permute-done
  187.8 7.9 collective-permute-start
  196.4 3.5 collective-permute-done
  212.4 7.9 collective-permute-start
  221.0 3.5 collective-permute-done
  237.0 7.9 collective-permute-start
  245.6 3.5 collective-permute-done
  261.6 7.9 collective-permute-start
  270.2 3.5 collective-permute-done
  286.2 7.9 collective-permute-start
  294.8 3.5 collective-permute-done
  310.7 7.9 collective-permute-start
  335.3 7.9 collective-permute-start
  343.9 3.5 collective-permute-done
  359.9 7.9 collective-permute-start
  368.5 3.5 collective-permute-done
  384.5 7.9 collective-permute-start
  409.1 7.9 collective-permute-start
  433.6 7.9 collective-permute-start
  442.2 3.5 collective-permute-done
  458.2 7.9 collective-permute-start
  466.8 3.5 collective-permute-done
  482.8 7.9 collective-permute-start
  491.4 3.5 collective-permute-done
  507.4 7.9 collective-permute-start
  516.0 3.5 collective-permute-done
  532.0 7.9 collective-permute-start
  540.6 3.5 collective-permute-done
  556.5 7.9 collective-permute-start
  565.2 3.5 collective-permute-done
  581.1 7.9 collective-permute-start
  589.7 4.6 collective-permute-done
  606.8 7.9 collective-permute-start
  615.4 5.8 collective-permute-done
  633.7 7.9 collective-permute-start
  642.3 3.6 collective-permute-done
  653.3 4.5 bitcast_convert_fusion
  661.5 4.6 pad_maximum_fusion
  666.1 6.5 copy.14
  675.8 34.2 %all-gather = f32[131072]{0:T(1024)S(1)} all-gather(f32[4096]{0:T(1024)S(1)} %select_add_fusion.1), channel_id=2, replica_groups=mesh['section'=16,'fsdp'=32] {'fsdp'}, dimensions={0}, use_global_device_ids=true | all-gather | bytes 540672 | tf_op jit(solution)/shard_map/all_gather | solution.py:179
  710.8 86.0 %reduce-scatter.4.cloned.1.call-done = bf16[128,512]{1,0:T(8,128)(2,1)} async-done(((bf16[4096,512]{1,0:T(8,128)(2,1)}), bf16[128,512]{1,0:T(8,128)(2,1)}) %reduce-scatter.4.cloned.1.call-update) | async-done | bytes 131088
  (465 shorter events, 338.7 us)
Async XLA Ops:
  7.2 4.1 copy-start.4
  7.2 78.6 %all-gather.3.cloned.1.call-start = ((), (), s32[]{:S(2)}) async-start(), calls=%async_computation.1 | async-start | bytes 4866048 | tf_op jit(solution)/shard_map/all_gather | solution.py:63
  9.0 787.9 %reduce-scatter.4.cloned.1.call-start = ((), (), s32[]{:S(2)}) async-start(), calls=%async_computation.2 | async-start | bytes 4325376
  88.4 2.4 copy-start
  89.3 2.5 copy-start.5
  93.2 0.8 copy-start.6
  94.1 7.3 copy-start.7
  94.1 7.3 copy-start.8
  94.1 7.3 copy-start.9
  94.1 7.3 copy-start.10
  113.3 11.2 %collective-permute-start = (bf16[32,4096]{1,0:T(8,128)(2,1)}, bf16[32,4096]{1,0:T(8,128)(2,1)S(1)}, u32[]{:S(2)}, u32[]{:S(2)}) collective-permute-start(bf16[32,4096]{1,0:T(8,128)(2,1)} %fusion.145), channel_id=1, source_target_pairs={{32,0},{64,32},{96,64},{128,96},{160,128},{192,160},{224,192},{256... | collective-permute-start | bytes 786440 | tf_op jit(solution)/shard_map/while/body/eval_jaxpr/ppermute | solution.py:10
  124.5 0.7 copy-start.1
  137.0 13.3 %collective-permute-start = (bf16[32,4096]{1,0:T(8,128)(2,1)}, bf16[32,4096]{1,0:T(8,128)(2,1)S(1)}, u32[]{:S(2)}, u32[]{:S(2)}) collective-permute-start(bf16[32,4096]{1,0:T(8,128)(2,1)} %fusion.145), channel_id=1, source_target_pairs={{32,0},{64,32},{96,64},{128,96},{160,128},{192,160},{224,192},{256... | collective-permute-start | bytes 786440 | tf_op jit(solution)/shard_map/while/body/eval_jaxpr/ppermute | solution.py:10
  150.4 0.7 copy-start.1
  162.9 12.4 %collective-permute-start = (bf16[32,4096]{1,0:T(8,128)(2,1)}, bf16[32,4096]{1,0:T(8,128)(2,1)S(1)}, u32[]{:S(2)}, u32[]{:S(2)}) collective-permute-start(bf16[32,4096]{1,0:T(8,128)(2,1)} %fusion.145), channel_id=1, source_target_pairs={{32,0},{64,32},{96,64},{128,96},{160,128},{192,160},{224,192},{256... | collective-permute-start | bytes 786440 | tf_op jit(solution)/shard_map/while/body/eval_jaxpr/ppermute | solution.py:10
  175.3 0.7 copy-start.1
  187.8 12.1 %collective-permute-start = (bf16[32,4096]{1,0:T(8,128)(2,1)}, bf16[32,4096]{1,0:T(8,128)(2,1)S(1)}, u32[]{:S(2)}, u32[]{:S(2)}) collective-permute-start(bf16[32,4096]{1,0:T(8,128)(2,1)} %fusion.145), channel_id=1, source_target_pairs={{32,0},{64,32},{96,64},{128,96},{160,128},{192,160},{224,192},{256... | collective-permute-start | bytes 786440 | tf_op jit(solution)/shard_map/while/body/eval_jaxpr/ppermute | solution.py:10
  199.9 0.7 copy-start.1
  212.4 12.1 %collective-permute-start = (bf16[32,4096]{1,0:T(8,128)(2,1)}, bf16[32,4096]{1,0:T(8,128)(2,1)S(1)}, u32[]{:S(2)}, u32[]{:S(2)}) collective-permute-start(bf16[32,4096]{1,0:T(8,128)(2,1)} %fusion.145), channel_id=1, source_target_pairs={{32,0},{64,32},{96,64},{128,96},{160,128},{192,160},{224,192},{256... | collective-permute-start | bytes 786440 | tf_op jit(solution)/shard_map/while/body/eval_jaxpr/ppermute | solution.py:10
  224.5 0.7 copy-start.1
  237.0 12.1 %collective-permute-start = (bf16[32,4096]{1,0:T(8,128)(2,1)}, bf16[32,4096]{1,0:T(8,128)(2,1)S(1)}, u32[]{:S(2)}, u32[]{:S(2)}) collective-permute-start(bf16[32,4096]{1,0:T(8,128)(2,1)} %fusion.145), channel_id=1, source_target_pairs={{32,0},{64,32},{96,64},{128,96},{160,128},{192,160},{224,192},{256... | collective-permute-start | bytes 786440 | tf_op jit(solution)/shard_map/while/body/eval_jaxpr/ppermute | solution.py:10
  249.1 0.7 copy-start.1
  261.6 12.1 %collective-permute-start = (bf16[32,4096]{1,0:T(8,128)(2,1)}, bf16[32,4096]{1,0:T(8,128)(2,1)S(1)}, u32[]{:S(2)}, u32[]{:S(2)}) collective-permute-start(bf16[32,4096]{1,0:T(8,128)(2,1)} %fusion.145), channel_id=1, source_target_pairs={{32,0},{64,32},{96,64},{128,96},{160,128},{192,160},{224,192},{256... | collective-permute-start | bytes 786440 | tf_op jit(solution)/shard_map/while/body/eval_jaxpr/ppermute | solution.py:10
  273.7 0.7 copy-start.1
  286.2 12.1 %collective-permute-start = (bf16[32,4096]{1,0:T(8,128)(2,1)}, bf16[32,4096]{1,0:T(8,128)(2,1)S(1)}, u32[]{:S(2)}, u32[]{:S(2)}) collective-permute-start(bf16[32,4096]{1,0:T(8,128)(2,1)} %fusion.145), channel_id=1, source_target_pairs={{32,0},{64,32},{96,64},{128,96},{160,128},{192,160},{224,192},{256... | collective-permute-start | bytes 786440 | tf_op jit(solution)/shard_map/while/body/eval_jaxpr/ppermute | solution.py:10
  298.3 0.7 copy-start.1
  310.7 12.1 %collective-permute-start = (bf16[32,4096]{1,0:T(8,128)(2,1)}, bf16[32,4096]{1,0:T(8,128)(2,1)S(1)}, u32[]{:S(2)}, u32[]{:S(2)}) collective-permute-start(bf16[32,4096]{1,0:T(8,128)(2,1)} %fusion.145), channel_id=1, source_target_pairs={{32,0},{64,32},{96,64},{128,96},{160,128},{192,160},{224,192},{256... | collective-permute-start | bytes 786440 | tf_op jit(solution)/shard_map/while/body/eval_jaxpr/ppermute | solution.py:10
  322.8 0.7 copy-start.1
  335.3 12.1 %collective-permute-start = (bf16[32,4096]{1,0:T(8,128)(2,1)}, bf16[32,4096]{1,0:T(8,128)(2,1)S(1)}, u32[]{:S(2)}, u32[]{:S(2)}) collective-permute-start(bf16[32,4096]{1,0:T(8,128)(2,1)} %fusion.145), channel_id=1, source_target_pairs={{32,0},{64,32},{96,64},{128,96},{160,128},{192,160},{224,192},{256... | collective-permute-start | bytes 786440 | tf_op jit(solution)/shard_map/while/body/eval_jaxpr/ppermute | solution.py:10
  359.9 12.1 %collective-permute-start = (bf16[32,4096]{1,0:T(8,128)(2,1)}, bf16[32,4096]{1,0:T(8,128)(2,1)S(1)}, u32[]{:S(2)}, u32[]{:S(2)}) collective-permute-start(bf16[32,4096]{1,0:T(8,128)(2,1)} %fusion.145), channel_id=1, source_target_pairs={{32,0},{64,32},{96,64},{128,96},{160,128},{192,160},{224,192},{256... | collective-permute-start | bytes 786440 | tf_op jit(solution)/shard_map/while/body/eval_jaxpr/ppermute | solution.py:10
  384.5 12.1 %collective-permute-start = (bf16[32,4096]{1,0:T(8,128)(2,1)}, bf16[32,4096]{1,0:T(8,128)(2,1)S(1)}, u32[]{:S(2)}, u32[]{:S(2)}) collective-permute-start(bf16[32,4096]{1,0:T(8,128)(2,1)} %fusion.145), channel_id=1, source_target_pairs={{32,0},{64,32},{96,64},{128,96},{160,128},{192,160},{224,192},{256... | collective-permute-start | bytes 786440 | tf_op jit(solution)/shard_map/while/body/eval_jaxpr/ppermute | solution.py:10
  396.5 0.7 copy-start.1
  409.1 12.1 %collective-permute-start = (bf16[32,4096]{1,0:T(8,128)(2,1)}, bf16[32,4096]{1,0:T(8,128)(2,1)S(1)}, u32[]{:S(2)}, u32[]{:S(2)}) collective-permute-start(bf16[32,4096]{1,0:T(8,128)(2,1)} %fusion.145), channel_id=1, source_target_pairs={{32,0},{64,32},{96,64},{128,96},{160,128},{192,160},{224,192},{256... | collective-permute-start | bytes 786440 | tf_op jit(solution)/shard_map/while/body/eval_jaxpr/ppermute | solution.py:10
  433.6 12.1 %collective-permute-start = (bf16[32,4096]{1,0:T(8,128)(2,1)}, bf16[32,4096]{1,0:T(8,128)(2,1)S(1)}, u32[]{:S(2)}, u32[]{:S(2)}) collective-permute-start(bf16[32,4096]{1,0:T(8,128)(2,1)} %fusion.145), channel_id=1, source_target_pairs={{32,0},{64,32},{96,64},{128,96},{160,128},{192,160},{224,192},{256... | collective-permute-start | bytes 786440 | tf_op jit(solution)/shard_map/while/body/eval_jaxpr/ppermute | solution.py:10
  445.7 0.7 copy-start.1
  458.2 12.1 %collective-permute-start = (bf16[32,4096]{1,0:T(8,128)(2,1)}, bf16[32,4096]{1,0:T(8,128)(2,1)S(1)}, u32[]{:S(2)}, u32[]{:S(2)}) collective-permute-start(bf16[32,4096]{1,0:T(8,128)(2,1)} %fusion.145), channel_id=1, source_target_pairs={{32,0},{64,32},{96,64},{128,96},{160,128},{192,160},{224,192},{256... | collective-permute-start | bytes 786440 | tf_op jit(solution)/shard_map/while/body/eval_jaxpr/ppermute | solution.py:10
  470.3 0.7 copy-start.1
  482.8 12.1 %collective-permute-start = (bf16[32,4096]{1,0:T(8,128)(2,1)}, bf16[32,4096]{1,0:T(8,128)(2,1)S(1)}, u32[]{:S(2)}, u32[]{:S(2)}) collective-permute-start(bf16[32,4096]{1,0:T(8,128)(2,1)} %fusion.145), channel_id=1, source_target_pairs={{32,0},{64,32},{96,64},{128,96},{160,128},{192,160},{224,192},{256... | collective-permute-start | bytes 786440 | tf_op jit(solution)/shard_map/while/body/eval_jaxpr/ppermute | solution.py:10
  507.4 12.1 %collective-permute-start = (bf16[32,4096]{1,0:T(8,128)(2,1)}, bf16[32,4096]{1,0:T(8,128)(2,1)S(1)}, u32[]{:S(2)}, u32[]{:S(2)}) collective-permute-start(bf16[32,4096]{1,0:T(8,128)(2,1)} %fusion.145), channel_id=1, source_target_pairs={{32,0},{64,32},{96,64},{128,96},{160,128},{192,160},{224,192},{256... | collective-permute-start | bytes 786440 | tf_op jit(solution)/shard_map/while/body/eval_jaxpr/ppermute | solution.py:10
  532.0 12.1 %collective-permute-start = (bf16[32,4096]{1,0:T(8,128)(2,1)}, bf16[32,4096]{1,0:T(8,128)(2,1)S(1)}, u32[]{:S(2)}, u32[]{:S(2)}) collective-permute-start(bf16[32,4096]{1,0:T(8,128)(2,1)} %fusion.145), channel_id=1, source_target_pairs={{32,0},{64,32},{96,64},{128,96},{160,128},{192,160},{224,192},{256... | collective-permute-start | bytes 786440 | tf_op jit(solution)/shard_map/while/body/eval_jaxpr/ppermute | solution.py:10
  556.5 12.1 %collective-permute-start = (bf16[32,4096]{1,0:T(8,128)(2,1)}, bf16[32,4096]{1,0:T(8,128)(2,1)S(1)}, u32[]{:S(2)}, u32[]{:S(2)}) collective-permute-start(bf16[32,4096]{1,0:T(8,128)(2,1)} %fusion.145), channel_id=1, source_target_pairs={{32,0},{64,32},{96,64},{128,96},{160,128},{192,160},{224,192},{256... | collective-permute-start | bytes 786440 | tf_op jit(solution)/shard_map/while/body/eval_jaxpr/ppermute | solution.py:10
  581.1 13.2 %collective-permute-start = (bf16[32,4096]{1,0:T(8,128)(2,1)}, bf16[32,4096]{1,0:T(8,128)(2,1)S(1)}, u32[]{:S(2)}, u32[]{:S(2)}) collective-permute-start(bf16[32,4096]{1,0:T(8,128)(2,1)} %fusion.145), channel_id=1, source_target_pairs={{32,0},{64,32},{96,64},{128,96},{160,128},{192,160},{224,192},{256... | collective-permute-start | bytes 786440 | tf_op jit(solution)/shard_map/while/body/eval_jaxpr/ppermute | solution.py:10
  606.8 14.4 %collective-permute-start = (bf16[32,4096]{1,0:T(8,128)(2,1)}, bf16[32,4096]{1,0:T(8,128)(2,1)S(1)}, u32[]{:S(2)}, u32[]{:S(2)}) collective-permute-start(bf16[32,4096]{1,0:T(8,128)(2,1)} %fusion.145), channel_id=1, source_target_pairs={{32,0},{64,32},{96,64},{128,96},{160,128},{192,160},{224,192},{256... | collective-permute-start | bytes 786440 | tf_op jit(solution)/shard_map/while/body/eval_jaxpr/ppermute | solution.py:10
  621.2 0.7 copy-start.1
  633.7 12.2 %collective-permute-start = (bf16[32,4096]{1,0:T(8,128)(2,1)}, bf16[32,4096]{1,0:T(8,128)(2,1)S(1)}, u32[]{:S(2)}, u32[]{:S(2)}) collective-permute-start(bf16[32,4096]{1,0:T(8,128)(2,1)} %fusion.145), channel_id=1, source_target_pairs={{32,0},{64,32},{96,64},{128,96},{160,128},{192,160},{224,192},{256... | collective-permute-start | bytes 786440 | tf_op jit(solution)/shard_map/while/body/eval_jaxpr/ppermute | solution.py:10
  653.3 4.5 copy-start.2
  653.3 4.5 copy-start.3
  653.3 5.6 copy-start.11
  (9 other events, 6.3 us)
Sparse Core Ops, SparseCore 0:
  10.7 75.0 all-gather.2
  672.7 124.0 reduce-scatter.3
where the time goes:
time: 816 us; the launch traced here: 806 us
  waiting for transfers between devices  242 us (30%)
  matrix products  175 us (21%)
  starting transfers between devices  171 us (21%)
  other arithmetic  117 us (14%)
  local copies, waits for them, and re-layouts  51.6 us (6%)
  blocking collectives  34.2 us (4%)
  between operations  14.3 us (2%)
    ppermute x22, starting transfers between devices, passed_along(): lax.ppermute(value, axis, [(source, source + steps) for source in range(l...  171 us
    unnamed x3, waiting for transfers between devices  86.1 us
    ppermute x22, waiting for transfers between devices, passed_along(): lax.ppermute(value, axis, [(source, source + steps) for source in range(l...  83.5 us
    dot_general x46, matrix products, contract_cols(): lax.dot_general(left, right, (((1,), (1,)), ((), ())), preferred_element_...  72.5 us
    all_gather x1, waiting for transfers between devices, on_device(): lax.all_gather(packed, 'fsdp', axis=0, tiled=True)  72 us
    dot_general x48, matrix products, contract_rows(): lax.dot_general(left, right, (((0,), (0,)), ((), ())), preferred_element_...  44.7 us
    convert_element_type x22, other arithmetic, tick(): grad_out = (grad_in.astype(jnp.float32) + grad_x).astype(jnp.bfloat16)  42.2 us
    dynamic_update_slice x23, other arithmetic, tick(): grad_store = lax.dynamic_update_index_in_dim(grad_store, grad_in, slot, 0)  40.8 us
  transfers between devices with their start and end apart: 24, of which 24 were waited for; matrix products, arithmetic and copies ran while one was open for 3% of the time, Pallas kernels for 0%

commit v1 on v0

--- a/solution.py
+++ b/solution.py
@@ -60,9 +60,9 @@
     gain_rows = jnp.zeros((16, weights.shape[2]), jnp.bfloat16)
     gain_rows = lax.dynamic_update_slice(gain_rows, gain[0][None, :], (0, 0))
     packed = jnp.concatenate([weights[0], gain_rows], axis=0)
-    gathered = lax.all_gather(packed, "fsdp", axis=0, tiled=True).reshape(
-        groups, rows_here + 16, weights.shape[2]
-    )
+    gathered = jnp.concatenate(
+        lax.all_to_all(jnp.stack([packed] * lax.axis_size("fsdp")), "fsdp", 0, 0), axis=0
+    ).reshape(groups, rows_here + 16, weights.shape[2])
     w_full = gathered[:, :rows_here, :].reshape(groups * rows_here, weights.shape[2])
     gain_full = gathered[:, rows_here, :rows_here].reshape(groups * rows_here)
     wide_gain = gain_full.astype(jnp.float32)

time: 816 us -> 860 us (1.054)
  waiting for transfers between devices: 242 us -> 272 us
  starting transfers between devices: 171 us -> 183 us
    all_to_all x0 -> x1, waiting for transfers between devices: none -> 103 us  [on_device(): lax.all_to_all(jnp.stack([packed] * lax.axis_size('fsdp')), 'fsdp', 0, 0)]
    all_gather x1 -> x0, waiting for transfers between devices: 72 us -> none  [on_device(): lax.all_gather(packed, 'fsdp', axis=0, tiled=True)]
    all_to_all x0 -> x1, starting transfers between devices: none -> 11.6 us  [on_device(): lax.all_to_all(jnp.stack([packed] * lax.axis_size('fsdp')), 'fsdp', 0, 0)]
    unnamed x3 -> x2, waiting for transfers between devices: 86.1 us -> 85.4 us
where the time goes in v1:
time: 860 us; the launch traced here: 850 us
  waiting for transfers between devices  272 us (32%)
  starting transfers between devices  183 us (21%)
  matrix products  175 us (20%)
  other arithmetic  116 us (13%)
  local copies, waits for them, and re-layouts  53.4 us (6%)
  blocking collectives  35.3 us (4%)
  between operations  14.3 us (2%)
    ppermute x22, starting transfers between devices, passed_along(): lax.ppermute(value, axis, [(source, source + steps) for source in range(l...  171 us
    all_to_all x1, waiting for transfers between devices, on_device(): lax.all_to_all(jnp.stack([packed] * lax.axis_size('fsdp')), 'fsdp', 0, 0)  103 us
    unnamed x2, waiting for transfers between devices  85.4 us
    ppermute x22, waiting for transfers between devices, passed_along(): lax.ppermute(value, axis, [(source, source + steps) for source in range(l...  83.5 us
    dot_general x46, matrix products, contract_cols(): lax.dot_general(left, right, (((1,), (1,)), ((), ())), preferred_element_...  72.5 us
    dot_general x48, matrix products, contract_rows(): lax.dot_general(left, right, (((0,), (0,)), ((), ())), preferred_element_...  44.7 us
    convert_element_type x22, other arithmetic, tick(): grad_out = (grad_in.astype(jnp.float32) + grad_x).astype(jnp.bfloat16)  42.2 us
    dynamic_update_slice x23, other arithmetic, tick(): grad_store = lax.dynamic_update_index_in_dim(grad_store, grad_in, slot, 0)  40.7 us
  transfers between devices with their start and end apart: 24, of which 24 were waited for; matrix products, arithmetic and copies ran while one was open for 3% of the time, Pallas kernels for 0%

profile of v1, /device:TPU:4, one launch (start us, length us, event | category | flops | bytes accessed | tf_op | source)
XLA Modules:
  0.0 849.6 jit_solution(18164398618521084972)
XLA Ops:
  10.8 11.6 %all-to-all-start = ((bf16[32,144,512]{2,1,0:T(8,128)(2,1)}), bf16[32,144,512]{2,1,0:T(8,128)(2,1)}, u32[]{:S(2)}, u32[]{:S(2)}) async-start(bf16[32,144,512]{2,1,0:T(8,128)(2,1)} %stack.2), calls=%async_computation | async-start | bytes 9437184 | tf_op jit(solution)/shard_map/all_to_all | solution.py:64
  25.7 103.3 %all-to-all-done = bf16[32,144,512]{2,1,0:T(8,128)(2,1)} async-done(((bf16[32,144,512]{2,1,0:T(8,128)(2,1)}), bf16[32,144,512]{2,1,0:T(8,128)(2,1)}, u32[]{:S(2)}, u32[]{:S(2)}) %all-to-all-start) | async-done | bytes 4718624 | tf_op jit(solution)/shard_map/all_to_all | solution.py:64
  144.5 545.7 %while.25 = (s32[]{:T(128)}, bf16[32,4096]{1,0:T(8,128)(2,1)}, bf16[10,32,4096]{2,1,0:T(8,128)(2,1)}, bf16[10,32,384]{2,1,0:T(8,128)(2,1)}, f32[4096]{0:T(1024)S...) while((s32[]{:T(128)}, bf16[32,4096]{1,0:T(8,128)(2,1)}, ...), condition=%wide.region_7.8_spmd.clone.clone.clone.clone, body=%wide.region_3.7_spmd.clone.clone.clone.clone.sunk | while | flops 137027552 | bytes 10679635 | solution.py:158
  156.3 5.6 collective-permute-start
  162.6 4.7 collective-permute-done
  179.9 7.9 collective-permute-start
  188.5 3.8 collective-permute-done
  204.8 7.9 collective-permute-start
  213.4 3.5 collective-permute-done
  229.4 7.9 collective-permute-start
  254.0 7.9 collective-permute-start
  278.5 7.9 collective-permute-start
  287.2 3.5 collective-permute-done
  303.1 7.9 collective-permute-start
  327.7 7.9 collective-permute-start
  336.3 3.5 collective-permute-done
  352.3 7.9 collective-permute-start
  360.8 3.5 collective-permute-done
  376.8 7.9 collective-permute-start
  385.4 3.5 collective-permute-done
  401.4 7.9 collective-permute-start
  410.0 3.5 collective-permute-done
  426.0 7.9 collective-permute-start
  434.6 3.5 collective-permute-done
  450.6 7.9 collective-permute-start
  459.2 3.5 collective-permute-done
  475.2 7.9 collective-permute-start
  499.8 7.9 collective-permute-start
  508.4 3.5 collective-permute-done
  524.3 7.9 collective-permute-start
  533.0 3.5 collective-permute-done
  548.9 7.9 collective-permute-start
  557.5 3.5 collective-permute-done
  573.5 7.9 collective-permute-start
  582.1 3.5 collective-permute-done
  598.1 7.9 collective-permute-start
  606.7 4.5 collective-permute-done
  623.8 7.9 collective-permute-start
  632.4 5.8 collective-permute-done
  650.6 7.9 collective-permute-start
  659.2 5.7 collective-permute-done
  677.4 7.9 collective-permute-start
  686.0 3.5 collective-permute-done
  696.9 4.5 bitcast_convert_fusion
  705.1 4.6 pad_maximum_fusion
  709.7 6.5 copy.14
  719.4 35.3 %all-gather = f32[131072]{0:T(1024)S(1)} all-gather(f32[4096]{0:T(1024)S(1)} %select_add_fusion.1), channel_id=2, replica_groups=mesh['section'=16,'fsdp'=32] {'fsdp'}, dimensions={0}, use_global_device_ids=true | all-gather | bytes 540672 | tf_op jit(solution)/shard_map/all_gather | solution.py:179
  755.5 85.4 %reduce-scatter.4.cloned.1.call-done = bf16[128,512]{1,0:T(8,128)(2,1)} async-done(((bf16[4096,512]{1,0:T(8,128)(2,1)}), bf16[128,512]{1,0:T(8,128)(2,1)}) %reduce-scatter.4.cloned.1.call-update) | async-done | bytes 131088
  (465 shorter events, 342.2 us)
Async XLA Ops:
  10.8 11.7 %copy-start.4 = (bf16[1,8,32,4096]{3,2,1,0:T(8,128)(2,1)S(1)}, bf16[1,8,32,4096]{3,2,1,0:T(8,128)(2,1)}, u32[]{:S(2)}) copy-start(bf16[1,8,32,4096]{3,2,1,0:T(8,128)(2,1)} %param.6) | copy-start | bytes 6291460
  10.8 118.2 %all-to-all-start = ((bf16[32,144,512]{2,1,0:T(8,128)(2,1)}), bf16[32,144,512]{2,1,0:T(8,128)(2,1)}, u32[]{:S(2)}, u32[]{:S(2)}) async-start(bf16[32,144,512]{2,1,0:T(8,128)(2,1)} %stack.2), calls=%async_computation | async-start | bytes 9437184 | tf_op jit(solution)/shard_map/all_to_all | solution.py:64
  22.4 818.5 %reduce-scatter.4.cloned.1.call-start = ((), (), s32[]{:S(2)}) async-start(), calls=%async_computation.2 | async-start | bytes 4325376
  131.7 3.1 copy-start
  131.7 3.1 copy-start.5
  136.1 0.8 copy-start.6
  137.0 7.4 copy-start.7
  137.1 7.4 copy-start.8
  137.1 7.4 copy-start.9
  137.1 7.4 copy-start.10
  156.3 11.1 %collective-permute-start = (bf16[32,4096]{1,0:T(8,128)(2,1)}, bf16[32,4096]{1,0:T(8,128)(2,1)S(1)}, u32[]{:S(2)}, u32[]{:S(2)}) collective-permute-start(bf16[32,4096]{1,0:T(8,128)(2,1)} %fusion.145), channel_id=1, source_target_pairs={{32,0},{64,32},{96,64},{128,96},{160,128},{192,160},{224,192},{256... | collective-permute-start | bytes 786440 | tf_op jit(solution)/shard_map/while/body/eval_jaxpr/ppermute | solution.py:10
  167.4 0.7 copy-start.1
  179.9 12.4 %collective-permute-start = (bf16[32,4096]{1,0:T(8,128)(2,1)}, bf16[32,4096]{1,0:T(8,128)(2,1)S(1)}, u32[]{:S(2)}, u32[]{:S(2)}) collective-permute-start(bf16[32,4096]{1,0:T(8,128)(2,1)} %fusion.145), channel_id=1, source_target_pairs={{32,0},{64,32},{96,64},{128,96},{160,128},{192,160},{224,192},{256... | collective-permute-start | bytes 786440 | tf_op jit(solution)/shard_map/while/body/eval_jaxpr/ppermute | solution.py:10
  192.3 0.7 copy-start.1
  204.8 12.1 %collective-permute-start = (bf16[32,4096]{1,0:T(8,128)(2,1)}, bf16[32,4096]{1,0:T(8,128)(2,1)S(1)}, u32[]{:S(2)}, u32[]{:S(2)}) collective-permute-start(bf16[32,4096]{1,0:T(8,128)(2,1)} %fusion.145), channel_id=1, source_target_pairs={{32,0},{64,32},{96,64},{128,96},{160,128},{192,160},{224,192},{256... | collective-permute-start | bytes 786440 | tf_op jit(solution)/shard_map/while/body/eval_jaxpr/ppermute | solution.py:10
  216.9 0.7 copy-start.1
  229.4 12.1 %collective-permute-start = (bf16[32,4096]{1,0:T(8,128)(2,1)}, bf16[32,4096]{1,0:T(8,128)(2,1)S(1)}, u32[]{:S(2)}, u32[]{:S(2)}) collective-permute-start(bf16[32,4096]{1,0:T(8,128)(2,1)} %fusion.145), channel_id=1, source_target_pairs={{32,0},{64,32},{96,64},{128,96},{160,128},{192,160},{224,192},{256... | collective-permute-start | bytes 786440 | tf_op jit(solution)/shard_map/while/body/eval_jaxpr/ppermute | solution.py:10
  241.5 0.7 copy-start.1
  254.0 12.1 %collective-permute-start = (bf16[32,4096]{1,0:T(8,128)(2,1)}, bf16[32,4096]{1,0:T(8,128)(2,1)S(1)}, u32[]{:S(2)}, u32[]{:S(2)}) collective-permute-start(bf16[32,4096]{1,0:T(8,128)(2,1)} %fusion.145), channel_id=1, source_target_pairs={{32,0},{64,32},{96,64},{128,96},{160,128},{192,160},{224,192},{256... | collective-permute-start | bytes 786440 | tf_op jit(solution)/shard_map/while/body/eval_jaxpr/ppermute | solution.py:10
  266.0 0.7 copy-start.1
  278.5 12.1 %collective-permute-start = (bf16[32,4096]{1,0:T(8,128)(2,1)}, bf16[32,4096]{1,0:T(8,128)(2,1)S(1)}, u32[]{:S(2)}, u32[]{:S(2)}) collective-permute-start(bf16[32,4096]{1,0:T(8,128)(2,1)} %fusion.145), channel_id=1, source_target_pairs={{32,0},{64,32},{96,64},{128,96},{160,128},{192,160},{224,192},{256... | collective-permute-start | bytes 786440 | tf_op jit(solution)/shard_map/while/body/eval_jaxpr/ppermute | solution.py:10
  290.6 0.7 copy-start.1
  303.1 12.1 %collective-permute-start = (bf16[32,4096]{1,0:T(8,128)(2,1)}, bf16[32,4096]{1,0:T(8,128)(2,1)S(1)}, u32[]{:S(2)}, u32[]{:S(2)}) collective-permute-start(bf16[32,4096]{1,0:T(8,128)(2,1)} %fusion.145), channel_id=1, source_target_pairs={{32,0},{64,32},{96,64},{128,96},{160,128},{192,160},{224,192},{256... | collective-permute-start | bytes 786440 | tf_op jit(solution)/shard_map/while/body/eval_jaxpr/ppermute | solution.py:10
  315.2 0.7 copy-start.1
  327.7 12.1 %collective-permute-start = (bf16[32,4096]{1,0:T(8,128)(2,1)}, bf16[32,4096]{1,0:T(8,128)(2,1)S(1)}, u32[]{:S(2)}, u32[]{:S(2)}) collective-permute-start(bf16[32,4096]{1,0:T(8,128)(2,1)} %fusion.145), channel_id=1, source_target_pairs={{32,0},{64,32},{96,64},{128,96},{160,128},{192,160},{224,192},{256... | collective-permute-start | bytes 786440 | tf_op jit(solution)/shard_map/while/body/eval_jaxpr/ppermute | solution.py:10
  339.8 0.7 copy-start.1
  352.3 12.1 %collective-permute-start = (bf16[32,4096]{1,0:T(8,128)(2,1)}, bf16[32,4096]{1,0:T(8,128)(2,1)S(1)}, u32[]{:S(2)}, u32[]{:S(2)}) collective-permute-start(bf16[32,4096]{1,0:T(8,128)(2,1)} %fusion.145), channel_id=1, source_target_pairs={{32,0},{64,32},{96,64},{128,96},{160,128},{192,160},{224,192},{256... | collective-permute-start | bytes 786440 | tf_op jit(solution)/shard_map/while/body/eval_jaxpr/ppermute | solution.py:10
  364.3 0.7 copy-start.1
  376.8 12.1 %collective-permute-start = (bf16[32,4096]{1,0:T(8,128)(2,1)}, bf16[32,4096]{1,0:T(8,128)(2,1)S(1)}, u32[]{:S(2)}, u32[]{:S(2)}) collective-permute-start(bf16[32,4096]{1,0:T(8,128)(2,1)} %fusion.145), channel_id=1, source_target_pairs={{32,0},{64,32},{96,64},{128,96},{160,128},{192,160},{224,192},{256... | collective-permute-start | bytes 786440 | tf_op jit(solution)/shard_map/while/body/eval_jaxpr/ppermute | solution.py:10
  388.9 0.7 copy-start.1
  401.4 12.1 %collective-permute-start = (bf16[32,4096]{1,0:T(8,128)(2,1)}, bf16[32,4096]{1,0:T(8,128)(2,1)S(1)}, u32[]{:S(2)}, u32[]{:S(2)}) collective-permute-start(bf16[32,4096]{1,0:T(8,128)(2,1)} %fusion.145), channel_id=1, source_target_pairs={{32,0},{64,32},{96,64},{128,96},{160,128},{192,160},{224,192},{256... | collective-permute-start | bytes 786440 | tf_op jit(solution)/shard_map/while/body/eval_jaxpr/ppermute | solution.py:10
  426.0 12.1 %collective-permute-start = (bf16[32,4096]{1,0:T(8,128)(2,1)}, bf16[32,4096]{1,0:T(8,128)(2,1)S(1)}, u32[]{:S(2)}, u32[]{:S(2)}) collective-permute-start(bf16[32,4096]{1,0:T(8,128)(2,1)} %fusion.145), channel_id=1, source_target_pairs={{32,0},{64,32},{96,64},{128,96},{160,128},{192,160},{224,192},{256... | collective-permute-start | bytes 786440 | tf_op jit(solution)/shard_map/while/body/eval_jaxpr/ppermute | solution.py:10
  450.6 12.1 %collective-permute-start = (bf16[32,4096]{1,0:T(8,128)(2,1)}, bf16[32,4096]{1,0:T(8,128)(2,1)S(1)}, u32[]{:S(2)}, u32[]{:S(2)}) collective-permute-start(bf16[32,4096]{1,0:T(8,128)(2,1)} %fusion.145), channel_id=1, source_target_pairs={{32,0},{64,32},{96,64},{128,96},{160,128},{192,160},{224,192},{256... | collective-permute-start | bytes 786440 | tf_op jit(solution)/shard_map/while/body/eval_jaxpr/ppermute | solution.py:10
  475.2 12.1 %collective-permute-start = (bf16[32,4096]{1,0:T(8,128)(2,1)}, bf16[32,4096]{1,0:T(8,128)(2,1)S(1)}, u32[]{:S(2)}, u32[]{:S(2)}) collective-permute-start(bf16[32,4096]{1,0:T(8,128)(2,1)} %fusion.145), channel_id=1, source_target_pairs={{32,0},{64,32},{96,64},{128,96},{160,128},{192,160},{224,192},{256... | collective-permute-start | bytes 786440 | tf_op jit(solution)/shard_map/while/body/eval_jaxpr/ppermute | solution.py:10
  487.3 0.7 copy-start.1
  499.8 12.1 %collective-permute-start = (bf16[32,4096]{1,0:T(8,128)(2,1)}, bf16[32,4096]{1,0:T(8,128)(2,1)S(1)}, u32[]{:S(2)}, u32[]{:S(2)}) collective-permute-start(bf16[32,4096]{1,0:T(8,128)(2,1)} %fusion.145), channel_id=1, source_target_pairs={{32,0},{64,32},{96,64},{128,96},{160,128},{192,160},{224,192},{256... | collective-permute-start | bytes 786440 | tf_op jit(solution)/shard_map/while/body/eval_jaxpr/ppermute | solution.py:10
  524.3 12.1 %collective-permute-start = (bf16[32,4096]{1,0:T(8,128)(2,1)}, bf16[32,4096]{1,0:T(8,128)(2,1)S(1)}, u32[]{:S(2)}, u32[]{:S(2)}) collective-permute-start(bf16[32,4096]{1,0:T(8,128)(2,1)} %fusion.145), channel_id=1, source_target_pairs={{32,0},{64,32},{96,64},{128,96},{160,128},{192,160},{224,192},{256... | collective-permute-start | bytes 786440 | tf_op jit(solution)/shard_map/while/body/eval_jaxpr/ppermute | solution.py:10
  548.9 12.1 %collective-permute-start = (bf16[32,4096]{1,0:T(8,128)(2,1)}, bf16[32,4096]{1,0:T(8,128)(2,1)S(1)}, u32[]{:S(2)}, u32[]{:S(2)}) collective-permute-start(bf16[32,4096]{1,0:T(8,128)(2,1)} %fusion.145), channel_id=1, source_target_pairs={{32,0},{64,32},{96,64},{128,96},{160,128},{192,160},{224,192},{256... | collective-permute-start | bytes 786440 | tf_op jit(solution)/shard_map/while/body/eval_jaxpr/ppermute | solution.py:10
  561.0 0.7 copy-start.1
  573.5 12.1 %collective-permute-start = (bf16[32,4096]{1,0:T(8,128)(2,1)}, bf16[32,4096]{1,0:T(8,128)(2,1)S(1)}, u32[]{:S(2)}, u32[]{:S(2)}) collective-permute-start(bf16[32,4096]{1,0:T(8,128)(2,1)} %fusion.145), channel_id=1, source_target_pairs={{32,0},{64,32},{96,64},{128,96},{160,128},{192,160},{224,192},{256... | collective-permute-start | bytes 786440 | tf_op jit(solution)/shard_map/while/body/eval_jaxpr/ppermute | solution.py:10
  598.1 13.2 %collective-permute-start = (bf16[32,4096]{1,0:T(8,128)(2,1)}, bf16[32,4096]{1,0:T(8,128)(2,1)S(1)}, u32[]{:S(2)}, u32[]{:S(2)}) collective-permute-start(bf16[32,4096]{1,0:T(8,128)(2,1)} %fusion.145), channel_id=1, source_target_pairs={{32,0},{64,32},{96,64},{128,96},{160,128},{192,160},{224,192},{256... | collective-permute-start | bytes 786440 | tf_op jit(solution)/shard_map/while/body/eval_jaxpr/ppermute | solution.py:10
  623.8 14.4 %collective-permute-start = (bf16[32,4096]{1,0:T(8,128)(2,1)}, bf16[32,4096]{1,0:T(8,128)(2,1)S(1)}, u32[]{:S(2)}, u32[]{:S(2)}) collective-permute-start(bf16[32,4096]{1,0:T(8,128)(2,1)} %fusion.145), channel_id=1, source_target_pairs={{32,0},{64,32},{96,64},{128,96},{160,128},{192,160},{224,192},{256... | collective-permute-start | bytes 786440 | tf_op jit(solution)/shard_map/while/body/eval_jaxpr/ppermute | solution.py:10
  638.1 0.7 copy-start.1
  650.6 14.3 %collective-permute-start = (bf16[32,4096]{1,0:T(8,128)(2,1)}, bf16[32,4096]{1,0:T(8,128)(2,1)S(1)}, u32[]{:S(2)}, u32[]{:S(2)}) collective-permute-start(bf16[32,4096]{1,0:T(8,128)(2,1)} %fusion.145), channel_id=1, source_target_pairs={{32,0},{64,32},{96,64},{128,96},{160,128},{192,160},{224,192},{256... | collective-permute-start | bytes 786440 | tf_op jit(solution)/shard_map/while/body/eval_jaxpr/ppermute | solution.py:10
  677.4 12.1 %collective-permute-start = (bf16[32,4096]{1,0:T(8,128)(2,1)}, bf16[32,4096]{1,0:T(8,128)(2,1)S(1)}, u32[]{:S(2)}, u32[]{:S(2)}) collective-permute-start(bf16[32,4096]{1,0:T(8,128)(2,1)} %fusion.145), channel_id=1, source_target_pairs={{32,0},{64,32},{96,64},{128,96},{160,128},{192,160},{224,192},{256... | collective-permute-start | bytes 786440 | tf_op jit(solution)/shard_map/while/body/eval_jaxpr/ppermute | solution.py:10
  696.9 4.5 copy-start.2
  696.9 4.5 copy-start.3
  696.9 5.6 copy-start.11
  (9 other events, 6.3 us)
Sparse Core Ops, SparseCore 0:
  716.3 124.5 reduce-scatter.3
